TPU v7x, 512 devices: a whole 4x4x16 slice. The times are simulated.
512 devices in a mesh: grp: 16 (over z_lo, core), row: 32 (over x, y, z_hi).
Axes of the slice: x: 4, y: 4, z: 16 (z_hi: 2, z_lo: 8; z = z_hi * 8 + z_lo), core: 2. Of those that a mesh axis runs over, the one named last changes fastest.
Arguments:
- signal: bfloat16 [2048, 64, 128], P(('grp', 'row')), may hold values from -6 to 6
- leaf_basis: bfloat16 [2048, 64, 128], P(('grp', 'row')), may hold values from -0.5 to 0.5
- near_blocks: bfloat16 [2048, 3, 128, 128], P(('grp', 'row')), may hold values from -0.3125 to 0.3125
- coupling: bfloat16 [98304, 4096], P(('grp', 'row')), may hold values from -0.109375 to 0.109375
- block_cols: int32 [98304], P(('grp', 'row')), may hold values from 0 to 2047, as said below
- block_rows: int32 [98304], P(('grp', 'row')), may hold values from 0 to 3
- block_live: int32 [98304], P(('grp', 'row')), may hold values 0 or 1
Outputs:
- product: bfloat16 [2048, 64, 128], P(('grp', 'row'))
Inputs may be any that keep to these rules, and one draw needn't show every extreme that they name: `block_cols`: slot b of device d (d = b // 192, in group h = d // 32) names a column cluster of group (h + o) mod (16), where o = (b mod 192) // 64 - 1; a group's clusters are g * 128 to (g + 1) * 128 - 1.
All inputs are finite; a program needn't handle non-finite values. No bound on the sum of `block_live` on one device may be relied on, other than what follows from the above.
Results may differ from a plain program's by a relative error of at most 0.0039.
Values may be sent and summed in bfloat16 or wider, within the bound.
A program may use at most 64 MiB of HBM per device.

v0:
```python
import jax
import jax.numpy as jnp
from jax import lax
from jax.sharding import PartitionSpec as P

K = 64
R = 64


def with_halo(block, sides, width, periodic):
    for axis, dim in sides:
        count = lax.axis_size(axis)
        forward = [(i, i + 1) for i in range(count - 1)]
        if periodic:
            forward.append((count - 1, 0))
        backward = [(target, source) for source, target in forward]
        low = lax.ppermute(
            lax.slice_in_dim(block, block.shape[dim] - width, None, axis=dim), axis, forward
        )
        high = lax.ppermute(lax.slice_in_dim(block, 0, width, axis=dim), axis, backward)
        block = jnp.concatenate([low, block, high], axis=dim)
    return block


def per_device(signal, leaf_basis, near_blocks, coupling, block_cols, block_rows, block_live):
    cl_dev = signal.shape[0]
    skeleton = jnp.einsum(
        "crl,ckl->crk", signal, leaf_basis, preferred_element_type=jnp.float32
    ).astype(jnp.bfloat16)
    flat_skel = skeleton.reshape(cl_dev, R * K)
    n_row = lax.axis_size("row")
    n_grp = lax.axis_size("grp")
    group_size = cl_dev * n_row
    panel = lax.all_gather(flat_skel, "row", axis=0, tiled=True)
    window_panel = with_halo(panel, (("grp", 0),), group_size, True)
    my_group = lax.axis_index("grp")
    column_group = block_cols // group_size
    position = (column_group - my_group + 1 + n_grp) % n_grp
    local_ids = position * group_size + block_cols % group_size
    sources = window_panel[local_ids].reshape(-1, R, K)
    sources = sources * block_live.astype(jnp.bfloat16)[:, None, None]
    blocks = coupling.reshape(-1, K, K)
    far_rows = []
    for cluster in range(cl_dev):
        chosen = (block_rows == cluster).astype(jnp.bfloat16)
        masked = sources * chosen[:, None, None]
        far_rows.append(
            jnp.einsum("brm,bkm->rk", masked, blocks, preferred_element_type=jnp.float32)
        )
    far = jnp.stack(far_rows, axis=0)
    far_skeleton = far.astype(jnp.bfloat16)
    total = jnp.einsum("crk,ckl->crl", far_skeleton, leaf_basis, preferred_element_type=jnp.float32)
    padded = with_halo(signal, ((("grp", "row"), 0),), 1, False)
    for index in range(3):
        neighbour = padded[index : index + cl_dev]
        total = total + jnp.einsum(
            "crl,cml->crm", neighbour, near_blocks[:, index], preferred_element_type=jnp.float32
        )
    return total.astype(jnp.bfloat16)


def solution(mesh):
    in_specs = (
        P(("grp", "row"), None, None),
        P(("grp", "row"), None, None),
        P(("grp", "row"), None, None, None),
        P(("grp", "row"), None),
        P(("grp", "row")),
        P(("grp", "row")),
        P(("grp", "row")),
    )
    out_specs = P(("grp", "row"), None, None)
    return jax.shard_map(
        per_device, mesh=mesh, in_specs=in_specs, out_specs=out_specs, check_vma=False
    )
```

profile of v0, /device:TPU:2, one launch (start us, length us, event | category | flops | bytes accessed | tf_op | source)
XLA Modules:
  0.0 215.5 jit_solution(11796397899471478045)
XLA Ops:
  6.5 0.0 copy-start
  6.5 0.0 copy-start.5
  6.5 0.0 copy-start.9
  6.5 0.0 copy-start.4
  6.5 0.0 all-gather.3.cloned.1.call-start
  6.6 0.8 copy-done
  7.4 1.0 convolution_convert_fusion
  8.4 0.7 reshape.171
  9.1 0.0 all-gather.3.cloned.1.call-update
  9.1 117.6 %all-gather.3.cloned.1.call-done = bf16[32,4,4096]{2,1,0:T(4,128)(2,1)} async-done(((bf16[1,4,4096]{2,1,0:T(4,128)(2,1)}), bf16[32,4,4096]{2,1,0:T(4,128)(2,1)}) %all-gather.3.cloned.1.call-update) | async-done | bytes 1048592 | tf_op jit(solution)/shard_map/all_gather | solution.py:34
  126.7 1.3 reshape.172
  128.1 0.0 copy-start.1
  128.1 0.0 copy-start.8
  128.1 0.0 copy-start.7
  128.1 2.1 collective-permute-start
  130.2 10.2 %collective-permute-start.1 = (bf16[128,4096]{1,0:T(8,128)(2,1)S(1)}, bf16[128,4096]{1,0:T(8,128)(2,1)}, u32[]{:S(2)}, u32[]{:S(2)}) collective-permute-start(bf16[128,4096]{1,0:T(8,128)(2,1)S(1)} %reshape.172), channel_id=1, source_target_pairs={{32,0},{64,32},{96,64},{128,96},{160,128},{192,160},{224,192},{256... | collective-permute-start | bytes 3145736 | tf_op jit(solution)/shard_map/ppermute | solution.py:20
  140.4 0.0 copy-done.5
  140.4 1.9 collective-permute-start.2
  142.4 15.6 %collective-permute-start.3 = (bf16[1,64,128]{2,1,0:T(8,128)(2,1)S(1)}, bf16[1,64,128]{2,1,0:T(8,128)(2,1)S(1)}, u32[]{:S(2)}, u32[]{:S(2)}) collective-permute-start(bf16[1,64,128]{2,1,0:T(8,128)(2,1)S(1)} %get-tuple-element.9), channel_id=1, source_target_pairs={{1,0},{2,1},{3,2},{4,3},{5,4},{6,5},{7,6},{8,7},{9,8},{10,9},{11,1... | collective-permute-start | bytes 49160 | tf_op jit(solution)/shard_map/ppermute | solution.py:20
  158.0 0.0 copy-done.9
  158.1 0.0 copy-done.4
  158.1 2.5 %copy.36 = bf16[192,4096]{0,1:T(8,128)(2,1)} copy(bf16[192,4096]{1,0:T(8,128)(2,1)S(1)} %copy-done.4) | data formatting | bytes 3145728 | tf_op args[3]
  160.6 0.0 copy-done.8
  160.6 0.0 copy-done.7
  160.6 1.1 fusion.75
  161.7 0.0 collective-permute-done
  161.7 0.0 copy-done.1
  161.8 0.0 collective-permute-done.1
  161.8 2.0 pad_maximum_fusion
  163.8 2.7 %gather_fusion = bf16[192,4096]{1,0:T(8,128)(2,1)} fusion(bf16[384,4096]{1,0:T(8,128)(2,1)S(1)} %pad_maximum_fusion, s32[1024]{0:T(1024)S(1)} %pad_clamp_fusion), kind=kCustom, calls=%fused_computation | custom fusion | bytes 3146496 | tf_op jit(solution)/shard_map/gather | solution.py:40
  166.5 3.6 %multiply_multiply_fusion.3 = (bf16[192,4096]{1,0:T(8,128)(2,1)}, bf16[192,4096]{1,0:T(8,128)(2,1)}, bf16[192,4096]{1,0:T(8,128)(2,1)S(1)}, bf16[192,4096]{1,0:T(8,128)(2,1)S(1)}) fusion(bf16[192,4096]{1,0:T(8,128)(2,1)} %gather_fusion, bf16[192]{0:T(256)(128)(2,1)S(1)} %get-tuple-element.11, bf16[192]{0:T(256)(128)(2,1)S(1)} %convert_element_type.23, ...), kind=kLoop, calls=%fused_computation.34 | loop fusion | flops 3932160 | bytes 7866240 | tf_op jit(solution)/shard_map/mul | solution.py:46
  170.0 3.8 %copy.35 = bf16[192,4096]{0,1:T(8,128)(2,1)} copy(bf16[192,4096]{1,0:T(8,128)(2,1)} %get-tuple-element.5) | data formatting | bytes 3145728 | tf_op jit(solution)/shard_map/mul | solution.py:46
  173.9 3.8 %copy.39 = bf16[192,4096]{0,1:T(8,128)(2,1)} copy(bf16[192,4096]{1,0:T(8,128)(2,1)} %get-tuple-element.6) | data formatting | bytes 3145728 | tf_op jit(solution)/shard_map/mul | solution.py:46
  177.7 0.0 copy-start.2
  177.7 0.0 copy-start.3
  177.7 6.8 %fusion.54 = bf16[1,64,64]{2,1,0:T(8,128)(2,1)S(1)} fusion(bf16[192,64,64]{0,2,1:T(8,128)(2,1)} %bitcast.56, bf16[192,64,64]{0,2,1:T(8,128)(2,1)} %bitcast.60), kind=kOutput, calls=%fused_computation.27 | convolution fusion | flops 100667392 | bytes 3153920 | tf_op jit(solution)/shard_map/brm,bkm->rk/dot_general | solution.py:48
  184.5 0.0 copy-done.2
  184.5 0.0 copy-done.3
  184.6 4.4 %fusion.59 = bf16[1,64,64]{2,1,0:T(8,128)(2,1)S(1)} fusion(bf16[192,64,64]{0,2,1:T(8,128)(2,1)S(1)} %bitcast.59, bf16[192,64,64]{0,2,1:T(8,128)(2,1)S(1)} %bitcast.61), kind=kOutput, calls=%fused_computation.28 | convolution fusion | flops 100667392 | bytes 3153920 | tf_op jit(solution)/shard_map/brm,bkm->rk/dot_general | solution.py:48
  189.0 2.6 %copy.42 = bf16[192,4096]{0,1:T(8,128)(2,1)} copy(bf16[192,4096]{1,0:T(8,128)(2,1)S(1)} %get-tuple-element.7) | data formatting | bytes 3145728 | tf_op jit(solution)/shard_map/mul | solution.py:46
  191.6 6.6 %fusion.64 = bf16[1,64,64]{2,1,0:T(8,128)(2,1)S(1)} fusion(bf16[192,64,64]{0,2,1:T(8,128)(2,1)} %bitcast.57, bf16[192,64,64]{0,2,1:T(8,128)(2,1)} %bitcast.63), kind=kOutput, calls=%fused_computation.29 | convolution fusion | flops 100667392 | bytes 3153920 | tf_op jit(solution)/shard_map/brm,bkm->rk/dot_general | solution.py:48
  198.3 2.5 %copy.45 = bf16[192,4096]{0,1:T(8,128)(2,1)} copy(bf16[192,4096]{1,0:T(8,128)(2,1)S(1)} %get-tuple-element.8) | data formatting | bytes 3145728 | tf_op jit(solution)/shard_map/mul | solution.py:46
  200.7 0.0 copy-start.6
  200.7 6.7 %fusion.69 = bf16[1,64,64]{2,1,0:T(8,128)(2,1)S(1)} fusion(bf16[192,64,64]{0,2,1:T(8,128)(2,1)} %bitcast.58, bf16[192,64,64]{0,2,1:T(8,128)(2,1)} %bitcast.62), kind=kOutput, calls=%fused_computation.30 | convolution fusion | flops 100667392 | bytes 3153920 | tf_op jit(solution)/shard_map/brm,bkm->rk/dot_general | solution.py:48
  207.4 0.1 fusion.87
  207.6 0.0 collective-permute-done.2
  207.6 0.0 copy-done.6
  207.6 0.2 fusion.12
  207.8 0.0 collective-permute-done.3
  207.8 0.8 fusion.13
  (5 shorter events, 0.0 us)
Async XLA Ops:
  6.5 0.8 copy-start
  6.5 133.9 %copy-start.5 = (bf16[4,64,128]{2,1,0:T(8,128)(2,1)S(1)}, bf16[4,64,128]{2,1,0:T(8,128)(2,1)}, u32[]{:S(2)}) copy-start(bf16[4,64,128]{2,1,0:T(8,128)(2,1)} %param.7) | copy-start | bytes 196612
  6.5 151.5 %copy-start.9 = (s32[192]{0:T(256)S(1)}, s32[192]{0:T(256)}, u32[]{:S(2)}) copy-start(s32[192]{0:T(256)} %param.13) | copy-start | bytes 2308
  6.5 151.5 %copy-start.4 = (bf16[192,4096]{1,0:T(8,128)(2,1)S(1)}, bf16[192,4096]{1,0:T(8,128)(2,1)}, u32[]{:S(2)}) copy-start(bf16[192,4096]{1,0:T(8,128)(2,1)} %param.10) | copy-start | bytes 4718596
  6.5 120.2 %all-gather.3.cloned.1.call-start = ((), (), s32[]{:S(2)}) async-start(), calls=%async_computation | async-start | bytes 1081344 | tf_op jit(solution)/shard_map/all_gather | solution.py:34
  128.1 33.7 %copy-start.1 = (bf16[128,4096]{1,0:T(8,128)(2,1)}, bf16[128,4096]{1,0:T(8,128)(2,1)S(1)}, u32[]{:S(2)}) copy-start(bf16[128,4096]{1,0:T(8,128)(2,1)S(1)} %reshape.172) | copy-start | bytes 3145732
  128.1 32.5 %copy-start.8 = (s32[192]{0:T(256)S(1)}, s32[192]{0:T(256)}, u32[]{:S(2)}) copy-start(s32[192]{0:T(256)} %param.11) | copy-start | bytes 2308
  128.1 32.5 %copy-start.7 = (s32[192]{0:T(256)S(1)}, s32[192]{0:T(256)}, u32[]{:S(2)}) copy-start(s32[192]{0:T(256)} %param.12) | copy-start | bytes 2308
  128.1 33.6 %collective-permute-start = (bf16[128,4096]{1,0:T(8,128)(2,1)S(1)}, bf16[128,4096]{1,0:T(8,128)(2,1)}, u32[]{:S(2)}, u32[]{:S(2)}) collective-permute-start(bf16[128,4096]{1,0:T(8,128)(2,1)S(1)} %reshape.172), channel_id=1, source_target_pairs={{0,32},{32,64},{64,96},{96,128},{128,160},{160,192},{192,224},{224... | collective-permute-start | bytes 3145736 | tf_op jit(solution)/shard_map/ppermute | solution.py:17
  130.2 31.6 %collective-permute-start.1 = (bf16[128,4096]{1,0:T(8,128)(2,1)S(1)}, bf16[128,4096]{1,0:T(8,128)(2,1)}, u32[]{:S(2)}, u32[]{:S(2)}) collective-permute-start(bf16[128,4096]{1,0:T(8,128)(2,1)S(1)} %reshape.172), channel_id=1, source_target_pairs={{32,0},{64,32},{96,64},{128,96},{160,128},{192,160},{224,192},{256... | collective-permute-start | bytes 3145736 | tf_op jit(solution)/shard_map/ppermute | solution.py:20
  140.4 67.1 %collective-permute-start.2 = (bf16[1,64,128]{2,1,0:T(8,128)(2,1)S(1)}, bf16[1,64,128]{2,1,0:T(8,128)(2,1)S(1)}, u32[]{:S(2)}, u32[]{:S(2)}) collective-permute-start(bf16[1,64,128]{2,1,0:T(8,128)(2,1)S(1)} %get-tuple-element.10), channel_id=1, source_target_pairs={{0,1},{1,2},{2,3},{3,4},{4,5},{5,6},{6,7},{7,8},{8,9},{9,10},{10,1... | collective-permute-start | bytes 49160 | tf_op jit(solution)/shard_map/ppermute | solution.py:17
  142.4 65.4 %collective-permute-start.3 = (bf16[1,64,128]{2,1,0:T(8,128)(2,1)S(1)}, bf16[1,64,128]{2,1,0:T(8,128)(2,1)S(1)}, u32[]{:S(2)}, u32[]{:S(2)}) collective-permute-start(bf16[1,64,128]{2,1,0:T(8,128)(2,1)S(1)} %get-tuple-element.9), channel_id=1, source_target_pairs={{1,0},{2,1},{3,2},{4,3},{5,4},{6,5},{7,6},{8,7},{9,8},{10,9},{11,1... | collective-permute-start | bytes 49160 | tf_op jit(solution)/shard_map/ppermute | solution.py:20
  177.7 6.8 %copy-start.2 = (bf16[192,4096]{0,1:T(8,128)(2,1)S(1)}, bf16[192,4096]{0,1:T(8,128)(2,1)}, u32[]{:S(2)}) copy-start(bf16[192,4096]{0,1:T(8,128)(2,1)} %copy.36) | copy-start | bytes 4718596
  177.7 6.8 %copy-start.3 = (bf16[192,4096]{0,1:T(8,128)(2,1)S(1)}, bf16[192,4096]{0,1:T(8,128)(2,1)}, u32[]{:S(2)}) copy-start(bf16[192,4096]{0,1:T(8,128)(2,1)} %copy.39) | copy-start | bytes 4718596
  200.7 6.9 %copy-start.6 = (bf16[4,3,128,128]{3,2,1,0:T(8,128)(2,1)S(1)}, bf16[4,3,128,128]{3,2,1,0:T(8,128)(2,1)}, u32[]{:S(2)}) copy-start(bf16[4,3,128,128]{3,2,1,0:T(8,128)(2,1)} %param.9) | copy-start | bytes 1179652
Sparse Core Ops, SparseCore 0:
  11.7 115.0 all-gather.2
where the time goes:
time: 216 us; the launch traced here: 215 us
  waiting for transfers between devices  118 us (55%)
  starting transfers between devices  29.9 us (14%)
  matrix products  27.8 us (13%)
  local copies, waits for them, and re-layouts  20.9 us (10%)
  between operations  13.7 us (6%)
  other arithmetic  5.57 us (3%)
    all_gather x1, waiting for transfers between devices, per_device(): panel = lax.all_gather(flat_skel, 'row', axis=0, tiled=True)  118 us
    ppermute x2, starting transfers between devices, with_halo(): lax.ppermute(lax.slice_in_dim(block, 0, width, axis=dim), axis, backward)  25.9 us
    dot_general x4, matrix products, per_device(): jnp.einsum('brm,bkm->rk', masked, blocks, preferred_element_type=jnp.floa...  24.6 us
    mul x4, local copies, waits for them, and re-layouts, per_device(): masked = sources * chosen[:, None, None]  12.8 us
    unnamed x23, local copies, waits for them, and re-layouts  5.42 us
  transfers between devices with their start and end apart: 5, of which 1 were waited for; matrix products, arithmetic and copies ran while one was open for 23% of the time, Pallas kernels for 0%

commit v1 on v0

--- a/solution.py
+++ b/solution.py
@@ -2,6 +2,7 @@
 import jax.numpy as jnp
 from jax import lax
 from jax.sharding import PartitionSpec as P
+from jax.lax import all_to_all, axis_size
 
 K = 64
 R = 64
@@ -31,7 +32,19 @@
     n_row = lax.axis_size("row")
     n_grp = lax.axis_size("grp")
     group_size = cl_dev * n_row
-    panel = lax.all_gather(flat_skel, "row", axis=0, tiled=True)
+
+    def treat_joints(my_data, chip_axis, at_axis):
+        return jnp.concatenate(
+            all_to_all(
+                jnp.stack([my_data] * axis_size(chip_axis)),
+                axis_name=chip_axis,
+                split_axis=0,
+                concat_axis=0,
+            ),
+            axis=at_axis,
+        )
+
+    panel = treat_joints(flat_skel, "row", at_axis=0)
     window_panel = with_halo(panel, (("grp", 0),), group_size, True)
     my_group = lax.axis_index("grp")
     column_group = block_cols // group_size

time: 216 us -> 162 us (0.75)
  the two profiles are of different devices: /device:TPU:2 before, /device:TPU:1 now
where the time goes in v1:
time: 162 us; the launch traced here: 161 us
  starting transfers between devices  53.6 us (33%)
  blocking collectives  51.9 us (32%)
  matrix products  27.8 us (17%)
  local copies, waits for them, and re-layouts  22.1 us (14%)
  other arithmetic  5.55 us (3%)
    all_to_all x1, blocking collectives, treat_joints(): all_to_all(jnp.stack([my_data] * axis_size(chip_axis)), axis_name=chip_ax...  51.9 us
    ppermute x2, starting transfers between devices, with_halo(): lax.ppermute(lax.slice_in_dim(block, block.shape[dim] - width, None, axis...  35.3 us
    dot_general x4, matrix products, per_device(): jnp.einsum('brm,bkm->rk', masked, blocks, preferred_element_type=jnp.floa...  24.6 us
    ppermute x2, starting transfers between devices, with_halo(): lax.ppermute(lax.slice_in_dim(block, 0, width, axis=dim), axis, backward)  18.3 us
    mul x4, local copies, waits for them, and re-layouts, per_device(): masked = sources * chosen[:, None, None]  12.8 us
    unnamed x21, local copies, waits for them, and re-layouts  5.72 us
    mul x1, other arithmetic, per_device(): masked = sources * chosen[:, None, None]  3.54 us
  transfers between devices with their start and end apart: 4, of which 0 were waited for; matrix products, arithmetic and copies ran while one was open for 32% of the time, Pallas kernels for 0%

profile of v1, /device:TPU:1, one launch (start us, length us, event | category | flops | bytes accessed | tf_op | source)
XLA Modules:
  0.0 161.3 jit_solution(15960940029960990189)
XLA Ops:
  0.0 0.0 copy-start
  0.0 0.8 copy-done
  0.8 1.0 convolution_convert_fusion
  1.8 0.1 stack_reshape.2
  2.0 0.5 stack.23
  2.4 0.0 copy-start.4
  2.4 0.0 copy-start.9
  2.5 51.9 %all_to_all.5 = bf16[32,4,4096]{2,1,0:T(4,128)(2,1)S(1)} all-to-all(bf16[32,4,4096]{2,1,0:T(4,128)(2,1)S(1)} %stack.23), channel_id=1, replica_groups=mesh['grp'=16,'row'=32] {'row'}, dimensions={0} | all-to-all | bytes 2097152 | tf_op jit(solution)/shard_map/all_to_all | solution.py:38
  54.4 0.3 reshape.162
  54.6 0.0 copy-start.1
  54.6 0.0 copy-start.8
  54.7 0.0 copy-start.7
  54.7 33.2 %collective-permute-start = (bf16[128,4096]{1,0:T(8,128)(2,1)S(1)}, bf16[128,4096]{1,0:T(8,128)(2,1)S(1)}, u32[]{:S(2)}, u32[]{:S(2)}) collective-permute-start(bf16[128,4096]{1,0:T(8,128)(2,1)S(1)} %reshape.162), channel_id=1, source_target_pairs={{0,32},{32,64},{64,96},{96,128},{128,160},{160,192},{192,224},{224... | collective-permute-start | bytes 3145736 | tf_op jit(solution)/shard_map/ppermute | solution.py:18
  87.9 1.9 %collective-permute-start.1 = (bf16[128,4096]{1,0:T(8,128)(2,1)S(1)}, bf16[128,4096]{1,0:T(8,128)(2,1)}, u32[]{:S(2)}, u32[]{:S(2)}) collective-permute-start(bf16[128,4096]{1,0:T(8,128)(2,1)S(1)} %reshape.162), channel_id=1, source_target_pairs={{32,0},{64,32},{96,64},{128,96},{160,128},{192,160},{224,192},{256... | collective-permute-start | bytes 3145736 | tf_op jit(solution)/shard_map/ppermute | solution.py:21
  89.8 0.0 copy-done.4
  89.8 2.1 %collective-permute-start.2 = (bf16[1,64,128]{2,1,0:T(8,128)(2,1)S(1)}, bf16[1,64,128]{2,1,0:T(8,128)(2,1)S(1)}, u32[]{:S(2)}, u32[]{:S(2)}) collective-permute-start(bf16[1,64,128]{2,1,0:T(8,128)(2,1)S(1)} %get-tuple-element.10), channel_id=1, source_target_pairs={{0,1},{1,2},{2,3},{3,4},{4,5},{5,6},{6,7},{7,8},{8,9},{9,10},{10,1... | collective-permute-start | bytes 49160 | tf_op jit(solution)/shard_map/ppermute | solution.py:18
  92.0 16.4 %collective-permute-start.3 = (bf16[1,64,128]{2,1,0:T(8,128)(2,1)S(1)}, bf16[1,64,128]{2,1,0:T(8,128)(2,1)S(1)}, u32[]{:S(2)}, u32[]{:S(2)}) collective-permute-start(bf16[1,64,128]{2,1,0:T(8,128)(2,1)S(1)} %get-tuple-element.9), channel_id=1, source_target_pairs={{1,0},{2,1},{3,2},{4,3},{5,4},{6,5},{7,6},{8,7},{9,8},{10,9},{11,1... | collective-permute-start | bytes 49160 | tf_op jit(solution)/shard_map/ppermute | solution.py:21
  108.4 0.0 copy-done.9
  108.4 3.9 %copy.20 = bf16[192,4096]{0,1:T(8,128)(2,1)} copy(bf16[192,4096]{1,0:T(8,128)(2,1)} %param.10) | data formatting | bytes 3145728 | tf_op args[3]
  112.2 0.0 copy-done.8
  112.3 0.0 copy-done.7
  112.3 1.1 fusion.75
  113.4 0.0 collective-permute-done
  113.4 0.0 copy-done.1
  113.4 0.0 copy-start.5
  113.4 1.0 copy-done.5
  114.4 0.0 collective-permute-done.1
  114.4 2.0 %pad_maximum_fusion = bf16[384,4096]{1,0:T(8,128)(2,1)S(1)} fusion(bf16[128,4096]{1,0:T(8,128)(2,1)} %collective-permute-done.1, bf16[128,4096]{1,0:T(8,128)(2,1)} %copy-done.1, bf16[128,4096]{1,0:T(8,128)(2,1)} %copy-done.5), kind=kLoop, calls=%fused_computation.1 | loop fusion | flops 9437184 | bytes 6291456 | tf_op jit(solution)/shard_map/concatenate | solution.py:22
  116.4 2.7 %gather_fusion = bf16[192,4096]{1,0:T(8,128)(2,1)} fusion(bf16[384,4096]{1,0:T(8,128)(2,1)S(1)} %pad_maximum_fusion, s32[1024]{0:T(1024)S(1)} %pad_clamp_fusion), kind=kCustom, calls=%fused_computation | custom fusion | bytes 3146496 | tf_op jit(solution)/shard_map/gather | solution.py:53
  119.1 3.5 %multiply_multiply_fusion.3 = (bf16[192,4096]{1,0:T(8,128)(2,1)}, bf16[192,4096]{1,0:T(8,128)(2,1)}, bf16[192,4096]{1,0:T(8,128)(2,1)S(1)}, bf16[192,4096]{1,0:T(8,128)(2,1)S(1)}) fusion(bf16[192,4096]{1,0:T(8,128)(2,1)} %gather_fusion, bf16[192]{0:T(256)(128)(2,1)S(1)} %get-tuple-element.11, bf16[192]{0:T(256)(128)(2,1)S(1)} %convert_element_type.23, ...), kind=kLoop, calls=%fused_computation.34 | loop fusion | flops 3932160 | bytes 7866240 | tf_op jit(solution)/shard_map/mul | solution.py:59
  122.6 3.8 %copy.19 = bf16[192,4096]{0,1:T(8,128)(2,1)} copy(bf16[192,4096]{1,0:T(8,128)(2,1)} %get-tuple-element.5) | data formatting | bytes 3145728 | tf_op jit(solution)/shard_map/mul | solution.py:59
  126.5 3.8 %copy.23 = bf16[192,4096]{0,1:T(8,128)(2,1)} copy(bf16[192,4096]{1,0:T(8,128)(2,1)} %get-tuple-element.6) | data formatting | bytes 3145728 | tf_op jit(solution)/shard_map/mul | solution.py:59
  130.3 0.0 copy-start.2
  130.3 0.0 copy-start.3
  130.3 6.8 %fusion.54 = bf16[1,64,64]{2,1,0:T(8,128)(2,1)S(1)} fusion(bf16[192,64,64]{0,2,1:T(8,128)(2,1)} %bitcast.56, bf16[192,64,64]{0,2,1:T(8,128)(2,1)} %bitcast.60), kind=kOutput, calls=%fused_computation.27 | convolution fusion | flops 100667392 | bytes 3153920 | tf_op jit(solution)/shard_map/brm,bkm->rk/dot_general | solution.py:61
  137.1 0.0 copy-done.2
  137.2 0.0 copy-done.3
  137.2 4.4 %fusion.59 = bf16[1,64,64]{2,1,0:T(8,128)(2,1)S(1)} fusion(bf16[192,64,64]{0,2,1:T(8,128)(2,1)S(1)} %bitcast.59, bf16[192,64,64]{0,2,1:T(8,128)(2,1)S(1)} %bitcast.61), kind=kOutput, calls=%fused_computation.28 | convolution fusion | flops 100667392 | bytes 3153920 | tf_op jit(solution)/shard_map/brm,bkm->rk/dot_general | solution.py:61
  141.6 2.7 %copy.26 = bf16[192,4096]{0,1:T(8,128)(2,1)} copy(bf16[192,4096]{1,0:T(8,128)(2,1)S(1)} %get-tuple-element.7) | data formatting | bytes 3145728 | tf_op jit(solution)/shard_map/mul | solution.py:59
  144.2 6.6 %fusion.64 = bf16[1,64,64]{2,1,0:T(8,128)(2,1)S(1)} fusion(bf16[192,64,64]{0,2,1:T(8,128)(2,1)} %bitcast.57, bf16[192,64,64]{0,2,1:T(8,128)(2,1)} %bitcast.63), kind=kOutput, calls=%fused_computation.29 | convolution fusion | flops 100667392 | bytes 3153920 | tf_op jit(solution)/shard_map/brm,bkm->rk/dot_general | solution.py:61
  150.9 2.5 %copy.29 = bf16[192,4096]{0,1:T(8,128)(2,1)} copy(bf16[192,4096]{1,0:T(8,128)(2,1)S(1)} %get-tuple-element.8) | data formatting | bytes 3145728 | tf_op jit(solution)/shard_map/mul | solution.py:59
  153.4 0.0 copy-start.6
  153.4 6.7 %fusion.69 = bf16[1,64,64]{2,1,0:T(8,128)(2,1)S(1)} fusion(bf16[192,64,64]{0,2,1:T(8,128)(2,1)} %bitcast.58, bf16[192,64,64]{0,2,1:T(8,128)(2,1)} %bitcast.62), kind=kOutput, calls=%fused_computation.30 | convolution fusion | flops 100667392 | bytes 3153920 | tf_op jit(solution)/shard_map/brm,bkm->rk/dot_general | solution.py:61
  160.1 0.1 fusion.87
  160.2 0.0 collective-permute-done.2
  160.2 0.0 copy-done.6
  160.2 0.2 fusion.12
  160.4 0.0 collective-permute-done.3
  160.4 0.8 fusion.13
  (5 shorter events, 0.0 us)
Async XLA Ops:
  0.0 0.8 copy-start
  2.4 87.4 %copy-start.4 = (bf16[4,64,128]{2,1,0:T(8,128)(2,1)S(1)}, bf16[4,64,128]{2,1,0:T(8,128)(2,1)}, u32[]{:S(2)}) copy-start(bf16[4,64,128]{2,1,0:T(8,128)(2,1)} %param.7) | copy-start | bytes 196612
  2.4 105.9 %copy-start.9 = (s32[192]{0:T(256)S(1)}, s32[192]{0:T(256)}, u32[]{:S(2)}) copy-start(s32[192]{0:T(256)} %param.13) | copy-start | bytes 2308
  54.6 58.8 %copy-start.1 = (bf16[128,4096]{1,0:T(8,128)(2,1)}, bf16[128,4096]{1,0:T(8,128)(2,1)S(1)}, u32[]{:S(2)}) copy-start(bf16[128,4096]{1,0:T(8,128)(2,1)S(1)} %reshape.162) | copy-start | bytes 3145732
  54.6 57.6 %copy-start.8 = (s32[192]{0:T(256)S(1)}, s32[192]{0:T(256)}, u32[]{:S(2)}) copy-start(s32[192]{0:T(256)} %param.11) | copy-start | bytes 2308
  54.7 57.6 %copy-start.7 = (s32[192]{0:T(256)S(1)}, s32[192]{0:T(256)}, u32[]{:S(2)}) copy-start(s32[192]{0:T(256)} %param.12) | copy-start | bytes 2308
  54.7 58.7 %collective-permute-start = (bf16[128,4096]{1,0:T(8,128)(2,1)S(1)}, bf16[128,4096]{1,0:T(8,128)(2,1)S(1)}, u32[]{:S(2)}, u32[]{:S(2)}) collective-permute-start(bf16[128,4096]{1,0:T(8,128)(2,1)S(1)} %reshape.162), channel_id=1, source_target_pairs={{0,32},{32,64},{64,96},{96,128},{128,160},{160,192},{192,224},{224... | collective-permute-start | bytes 3145736 | tf_op jit(solution)/shard_map/ppermute | solution.py:18
  87.9 26.5 %collective-permute-start.1 = (bf16[128,4096]{1,0:T(8,128)(2,1)S(1)}, bf16[128,4096]{1,0:T(8,128)(2,1)}, u32[]{:S(2)}, u32[]{:S(2)}) collective-permute-start(bf16[128,4096]{1,0:T(8,128)(2,1)S(1)} %reshape.162), channel_id=1, source_target_pairs={{32,0},{64,32},{96,64},{128,96},{160,128},{192,160},{224,192},{256... | collective-permute-start | bytes 3145736 | tf_op jit(solution)/shard_map/ppermute | solution.py:21
  89.8 70.4 %collective-permute-start.2 = (bf16[1,64,128]{2,1,0:T(8,128)(2,1)S(1)}, bf16[1,64,128]{2,1,0:T(8,128)(2,1)S(1)}, u32[]{:S(2)}, u32[]{:S(2)}) collective-permute-start(bf16[1,64,128]{2,1,0:T(8,128)(2,1)S(1)} %get-tuple-element.10), channel_id=1, source_target_pairs={{0,1},{1,2},{2,3},{3,4},{4,5},{5,6},{6,7},{7,8},{8,9},{9,10},{10,1... | collective-permute-start | bytes 49160 | tf_op jit(solution)/shard_map/ppermute | solution.py:18
  92.0 68.5 %collective-permute-start.3 = (bf16[1,64,128]{2,1,0:T(8,128)(2,1)S(1)}, bf16[1,64,128]{2,1,0:T(8,128)(2,1)S(1)}, u32[]{:S(2)}, u32[]{:S(2)}) collective-permute-start(bf16[1,64,128]{2,1,0:T(8,128)(2,1)S(1)} %get-tuple-element.9), channel_id=1, source_target_pairs={{1,0},{2,1},{3,2},{4,3},{5,4},{6,5},{7,6},{8,7},{9,8},{10,9},{11,1... | collective-permute-start | bytes 49160 | tf_op jit(solution)/shard_map/ppermute | solution.py:21
  113.4 1.0 copy-start.5
  130.3 6.8 %copy-start.2 = (bf16[192,4096]{0,1:T(8,128)(2,1)S(1)}, bf16[192,4096]{0,1:T(8,128)(2,1)}, u32[]{:S(2)}) copy-start(bf16[192,4096]{0,1:T(8,128)(2,1)} %copy.20) | copy-start | bytes 4718596
  130.3 6.8 %copy-start.3 = (bf16[192,4096]{0,1:T(8,128)(2,1)S(1)}, bf16[192,4096]{0,1:T(8,128)(2,1)}, u32[]{:S(2)}) copy-start(bf16[192,4096]{0,1:T(8,128)(2,1)} %copy.23) | copy-start | bytes 4718596
  153.4 6.9 %copy-start.6 = (bf16[4,3,128,128]{3,2,1,0:T(8,128)(2,1)S(1)}, bf16[4,3,128,128]{3,2,1,0:T(8,128)(2,1)}, u32[]{:S(2)}) copy-start(bf16[4,3,128,128]{3,2,1,0:T(8,128)(2,1)} %param.9) | copy-start | bytes 1179652
